TPU v7x, 32 devices: a whole 2x2x4 slice. The times are simulated.
32 devices in a mesh: dp: 8 (over y, x, core), mp: 4 (over z).
Axes of the slice: x: 2, y: 2, z: 4, core: 2. Of those that a mesh axis runs over, the one named last changes fastest.
Arguments:
- token_ids: int32 [8192], P('dp'), may hold values from 0 to 8191
- segment_ids: int32 [8192], P('dp'), may hold values from 0 to 64, as said below
- timesteps: int32 [8], P('dp'), may hold values from 0 to 999
- token_table: bfloat16 [8192, 768], P(None, 'mp'), may hold values from -4.1875 to 4.1875
- time_table: bfloat16 [1000, 768], P(None, 'mp'), may hold values from -4.1875 to 4.1875
- ln1_gain: float32 [768], replicated, may hold values from 0.1 to 1.9
- ln1_bias: float32 [768], replicated, may hold values from -1.8 to 1.8
- w_qkv: bfloat16 [768, 3, 768], P(None, None, 'mp'), may hold values from -0.3125 to 0.3125
- w_out: bfloat16 [768, 768], P('mp'), may hold values from -1.25 to 1.25
- attn_bias: float32 [768], replicated, may hold values from -3 to 3
- ln2_gain: float32 [768], replicated, may hold values from 0.1 to 1.9
- ln2_bias: float32 [768], replicated, may hold values from -1.8 to 1.8
- w_up: bfloat16 [768, 3072], P(None, 'mp'), may hold values from -0.21875 to 0.21875
- w_down: bfloat16 [3072, 768], P('mp'), may hold values from -0.15625 to 0.15625
- mlp_bias: float32 [768], replicated, may hold values from -3 to 3
- cotangent: bfloat16 [8192, 768], P(('dp', 'mp')), may hold values from -6 to 6
Outputs:
- output: bfloat16 [8192, 768], P(('dp', 'mp'))
- input_grad: float32 [8192, 768], P(('dp', 'mp'))
- grad_token_table: float32 [8192, 768], P('dp', 'mp')
- grad_time_table: float32 [1000, 768], replicated
- grad_ln1_gain: float32 [768], replicated
- grad_ln1_bias: float32 [768], replicated
- grad_w_qkv: float32 [768, 3, 768], P('dp', None, 'mp')
- grad_w_out: float32 [768, 768], P('mp', 'dp')
- grad_attn_bias: float32 [768], replicated
- grad_ln2_gain: float32 [768], replicated
- grad_ln2_bias: float32 [768], replicated
- grad_w_up: float32 [768, 3072], P('dp', 'mp')
- grad_w_down: float32 [3072, 768], P('mp', 'dp')
- grad_mlp_bias: float32 [768], replicated
Inputs may be any that keep to these rules, and one draw needn't show every extreme that they name: `segment_ids`: within each sequence of 1024 tokens the ids start at 1 and rise by 0 or 1 from one token to the next; a tail of padding zeros may follow.
All inputs are finite; a program needn't handle non-finite values.
Results may differ from a plain program's by a relative error of at most 0.018.
The roundings to bfloat16 on the way count: a program that leaves them out, or rounds other values in their place, can miss the bound.
Values may be sent and summed in bfloat16 or wider, within the bound.
A program may use at most 128 MiB of HBM per device.

v0:
```python
import jax
import jax.numpy as jnp
from jax import lax
from jax.sharding import PartitionSpec as P

D = 768
HD = 64
L = 1024
QBLK = 512
PRECISE = lax.Precision.HIGHEST


def as_sent(array):
    return jax.tree.map(lambda a: a.astype(jnp.bfloat16) if a.dtype == jnp.float32 else a, array)


def layer_norm(stream, gain, shift):
    average = jnp.mean(stream, axis=-1, keepdims=True)
    centered = stream - average
    variance = jnp.mean(centered * centered, axis=-1, keepdims=True)
    return centered * lax.rsqrt(variance + 1e-05) * gain + shift


def allowed_pairs(seg_query, segments, first_row):
    key_pos = jnp.arange(L)
    query_pos = first_row + jnp.arange(QBLK)
    same_text = seg_query[:, None] == segments[None, :]
    self_or_text = (seg_query[:, None] != 0) | (query_pos[:, None] == key_pos[None, :])
    return same_text & self_or_text


def attend_forward(queries, key_rows, value_rows, segments):
    outputs = []
    log_parts = []
    for block_index in range(L // QBLK):
        first_row = block_index * QBLK
        query_block = queries[first_row : first_row + QBLK]
        allowed = allowed_pairs(segments[first_row : first_row + QBLK], segments, first_row)
        scores = (
            jnp.einsum("qhd,khd->hqk", query_block, key_rows, preferred_element_type=jnp.float32)
            * 0.125
        )
        masked = jnp.where(allowed[None], scores, -1e30)
        highest = jnp.max(masked, axis=-1, keepdims=True)
        exponents = jnp.exp(masked - highest)
        totals = jnp.sum(exponents, axis=-1, keepdims=True)
        weights = (exponents / totals).astype(jnp.bfloat16)
        outputs.append(
            jnp.einsum(
                "hqk,khd->qhd", weights, value_rows, preferred_element_type=jnp.float32
            ).astype(jnp.bfloat16)
        )
        log_parts.append((highest + jnp.log(totals))[..., 0])
    return (jnp.concatenate(outputs, axis=0), jnp.concatenate(log_parts, axis=1))


def attend_backward(queries, key_rows, value_rows, segments, log_sums, grad_heads):
    grad_keys = jnp.zeros(key_rows.shape, jnp.float32)
    grad_values = jnp.zeros(value_rows.shape, jnp.float32)
    grad_queries = []
    for block_index in range(L // QBLK):
        first_row = block_index * QBLK
        query_block = queries[first_row : first_row + QBLK]
        grad_block = grad_heads[first_row : first_row + QBLK]
        allowed = allowed_pairs(segments[first_row : first_row + QBLK], segments, first_row)
        scores = (
            jnp.einsum("qhd,khd->hqk", query_block, key_rows, preferred_element_type=jnp.float32)
            * 0.125
        )
        masked = jnp.where(allowed[None], scores, -1e30)
        probs = jnp.exp(masked - log_sums[:, first_row : first_row + QBLK, None])
        rounded = probs.astype(jnp.bfloat16)
        grad_probs = jnp.einsum(
            "qhd,khd->hqk", grad_block, value_rows, preferred_element_type=jnp.float32
        )
        inner = jnp.sum(probs * grad_probs, axis=-1, keepdims=True)
        grad_scores = (probs * (grad_probs - inner)).astype(jnp.bfloat16)
        grad_queries.append(
            jnp.einsum("hqk,khd->qhd", grad_scores, key_rows, preferred_element_type=jnp.float32)
            * 0.125
        )
        grad_keys = (
            grad_keys
            + jnp.einsum(
                "hqk,qhd->khd", grad_scores, query_block, preferred_element_type=jnp.float32
            )
            * 0.125
        )
        grad_values = grad_values + jnp.einsum(
            "hqk,qhd->khd", rounded, grad_block, preferred_element_type=jnp.float32
        )
    return (
        jnp.concatenate(grad_queries, axis=0).astype(jnp.bfloat16),
        grad_keys.astype(jnp.bfloat16),
        grad_values.astype(jnp.bfloat16),
    )


def block_forward(
    stream_in,
    segment_ids,
    ln1_gain,
    ln1_bias,
    w_qkv,
    w_out,
    attn_bias,
    ln2_gain,
    ln2_bias,
    w_up,
    w_down,
    mlp_bias,
):
    own_rows = stream_in.shape[0]
    normed_one = layer_norm(stream_in, ln1_gain, ln1_bias).astype(jnp.bfloat16)
    gathered_one = lax.all_gather(normed_one, "mp", axis=0, tiled=True)
    tokens_all = gathered_one.shape[0]
    local_width = w_qkv.shape[2]
    heads_local = local_width // HD
    packed = jnp.dot(
        gathered_one, w_qkv.reshape(D, 3 * local_width), preferred_element_type=jnp.float32
    ).astype(jnp.bfloat16)
    packed = packed.reshape(tokens_all // L, L, 3, heads_local, HD)
    queries = packed[:, :, 0]
    key_rows = packed[:, :, 1]
    value_rows = packed[:, :, 2]
    attended, log_sums = lax.map(
        lambda per_seq: attend_forward(per_seq[0], per_seq[1], per_seq[2], per_seq[3]),
        (queries, key_rows, value_rows, segment_ids.reshape(tokens_all // L, L)),
    )
    attended_flat = attended.reshape(tokens_all, local_width)
    attn_rows = lax.psum_scatter(
        jnp.dot(
            lax.slice_in_dim(attended_flat, 0, own_rows * lax.axis_size("mp"), axis=0),
            w_out,
            preferred_element_type=jnp.float32,
        ),
        "mp",
        scatter_dimension=0,
        tiled=True,
    )
    stream_mid = stream_in + attn_rows + attn_bias
    normed_two = layer_norm(stream_mid, ln2_gain, ln2_bias).astype(jnp.bfloat16)
    gathered_two = lax.all_gather(normed_two, "mp", axis=0, tiled=True)
    pre_act = jnp.dot(gathered_two, w_up, preferred_element_type=jnp.float32)
    activation = jax.nn.gelu(pre_act, approximate=True).astype(jnp.bfloat16)
    mlp_rows = lax.psum_scatter(
        jnp.dot(
            lax.slice_in_dim(activation, 0, own_rows * lax.axis_size("mp"), axis=0),
            w_down,
            preferred_element_type=jnp.float32,
        ).astype(jnp.bfloat16),
        "mp",
        scatter_dimension=0,
        tiled=True,
    ).astype(jnp.float32)
    output = stream_mid + mlp_rows + mlp_bias
    saved = (
        stream_mid,
        gathered_one,
        queries,
        key_rows,
        value_rows,
        attended_flat,
        log_sums,
        gathered_two,
        pre_act,
        activation,
    )
    return (output, saved)


def contract_rows(left, right):
    return lax.dot_general(
        left, right, (((0,), (0,)), ((), ())), preferred_element_type=jnp.float32
    )


def contract_cols(left, right):
    return lax.dot_general(
        left, right, (((1,), (1,)), ((), ())), preferred_element_type=jnp.float32
    )


def on_device(
    token_ids,
    segment_ids,
    timesteps,
    token_table,
    time_table,
    ln1_gain,
    ln1_bias,
    w_qkv,
    w_out,
    attn_bias,
    ln2_gain,
    ln2_bias,
    w_up,
    w_down,
    mlp_bias,
    cotangent,
):
    group_size = lax.axis_size("mp")
    member = lax.axis_index("mp")
    tokens_all = token_ids.shape[0]
    own_rows = tokens_all // group_size
    seq_count = timesteps.shape[0]
    local_width = token_table.shape[1]
    step_match = timesteps[:, None] == jnp.arange(time_table.shape[0])[None, :]
    time_rows = jnp.dot(
        step_match.astype(jnp.bfloat16), time_table, preferred_element_type=jnp.float32
    )
    embedded = (
        token_table[token_ids].astype(jnp.float32).reshape(seq_count, L, local_width)
        + time_rows[:, None, :]
    )
    stream_in = lax.all_to_all(
        embedded.reshape(tokens_all, local_width), "mp", split_axis=0, concat_axis=1, tiled=True
    )
    weights = (
        ln1_gain,
        ln1_bias,
        w_qkv,
        w_out,
        attn_bias,
        ln2_gain,
        ln2_bias,
        w_up,
        w_down,
        mlp_bias,
    )
    output, saved = block_forward(stream_in, segment_ids, *weights)
    repeated, saved = block_forward(lax.optimization_barrier(stream_in), segment_ids, *weights)
    (
        stream_mid,
        gathered_one,
        queries,
        key_rows,
        value_rows,
        attended_flat,
        log_sums,
        gathered_two,
        pre_act,
        activation,
    ) = saved
    own_segments = lax.dynamic_slice_in_dim(segment_ids, member * own_rows, own_rows, 0)
    grad_out = cotangent.astype(jnp.float32) * (own_segments != 0).astype(jnp.float32)[:, None]
    grad_mlp_bias = jnp.sum(grad_out, axis=0)
    grad_mlp_all = lax.all_gather(grad_out.astype(jnp.bfloat16), "mp", axis=0, tiled=True)
    grad_w_down = contract_rows(activation, grad_mlp_all)
    grad_act = contract_cols(grad_mlp_all, w_down)
    gelu_back = jax.vjp(lambda inner: jax.nn.gelu(inner, approximate=True), pre_act)[1]
    grad_pre = gelu_back(grad_act)[0].astype(jnp.bfloat16)
    grad_w_up = contract_rows(gathered_two, grad_pre)
    grad_norm_two = lax.psum_scatter(
        contract_cols(
            lax.slice_in_dim(grad_pre, 0, own_rows * lax.axis_size("mp"), axis=0), w_up
        ).astype(jnp.bfloat16),
        "mp",
        scatter_dimension=0,
        tiled=True,
    ).astype(jnp.float32)
    norm_back_two = jax.vjp(layer_norm, stream_mid, ln2_gain, ln2_bias)[1]
    grad_mid_norm, grad_ln2_gain, grad_ln2_bias = norm_back_two(grad_norm_two)
    grad_mid = grad_out + grad_mid_norm
    grad_attn_bias = jnp.sum(grad_mid, axis=0)
    grad_attn_all = lax.all_gather(grad_mid.astype(jnp.bfloat16), "mp", axis=0, tiled=True)
    grad_w_out = contract_rows(attended_flat, grad_attn_all)
    grad_attended = contract_cols(grad_attn_all, w_out).astype(jnp.bfloat16)
    heads_local = local_width // HD
    grad_heads = grad_attended.reshape(seq_count, L, heads_local, HD)
    grad_q, grad_k, grad_v = lax.map(
        lambda per_seq: attend_backward(
            per_seq[0], per_seq[1], per_seq[2], per_seq[3], per_seq[4], per_seq[5]
        ),
        (queries, key_rows, value_rows, segment_ids.reshape(seq_count, L), log_sums, grad_heads),
    )
    grad_packed = jnp.stack((grad_q, grad_k, grad_v), axis=2).reshape(tokens_all, 3 * local_width)
    grad_w_qkv = contract_rows(gathered_one, grad_packed).reshape(D, 3, local_width)
    qkv_flat = w_qkv.reshape(D, 3 * local_width)
    grad_norm_one = lax.psum_scatter(
        contract_cols(grad_packed, qkv_flat).astype(jnp.bfloat16),
        "mp",
        scatter_dimension=0,
        tiled=True,
    ).astype(jnp.float32)
    norm_back_one = jax.vjp(layer_norm, stream_in, ln1_gain, ln1_bias)[1]
    grad_in_norm, grad_ln1_gain, grad_ln1_bias = norm_back_one(grad_norm_one)
    input_grad = grad_mid + grad_in_norm
    grad_columns = lax.all_to_all(
        as_sent(input_grad), "mp", split_axis=1, concat_axis=0, tiled=True
    ).astype(input_grad.dtype)
    grad_token_table = (
        jnp.zeros((token_table.shape[0], local_width), jnp.float32).at[token_ids].add(grad_columns)
    )
    seq_of_row = (member * own_rows + jnp.arange(own_rows)) // L
    seq_onehot = (seq_of_row[:, None] == jnp.arange(seq_count)[None, :]).astype(jnp.float32)
    seq_sums = lax.dot_general(
        seq_onehot,
        input_grad,
        (((0,), (0,)), ((), ())),
        precision=PRECISE,
        preferred_element_type=jnp.float32,
    )
    grad_time_table = lax.dot_general(
        step_match.astype(jnp.float32),
        seq_sums,
        (((0,), (0,)), ((), ())),
        precision=PRECISE,
        preferred_element_type=jnp.float32,
    )
    small_sums = lax.psum(
        (
            grad_time_table,
            grad_ln1_gain,
            grad_ln1_bias,
            grad_attn_bias,
            grad_ln2_gain,
            grad_ln2_bias,
            grad_mlp_bias,
        ),
        ("dp", "mp"),
    )
    sum_qkv, sum_out, sum_up, sum_down, sum_token = (
        lax.psum_scatter(grad_w_qkv, "dp", scatter_dimension=0, tiled=True),
        lax.psum_scatter(grad_w_out, "dp", scatter_dimension=1, tiled=True),
        lax.psum_scatter(grad_w_up, "dp", scatter_dimension=0, tiled=True),
        lax.psum_scatter(grad_w_down, "dp", scatter_dimension=1, tiled=True),
        lax.psum_scatter(grad_token_table, "dp", scatter_dimension=0, tiled=True),
    )
    return (
        output.astype(jnp.bfloat16),
        input_grad,
        sum_token,
        small_sums[0],
        small_sums[1],
        small_sums[2],
        sum_qkv,
        sum_out,
        small_sums[3],
        small_sums[4],
        small_sums[5],
        sum_up,
        sum_down,
        small_sums[6],
    )


def solution(mesh):
    placed = (
        P("dp"),
        P("dp"),
        P("dp"),
        P(None, "mp"),
        P(None, "mp"),
        P(),
        P(),
        P(None, None, "mp"),
        P("mp", None),
        P(),
        P(),
        P(),
        P(None, "mp"),
        P("mp", None),
        P(),
        P(("dp", "mp"), None),
    )
    return jax.shard_map(
        on_device,
        mesh=mesh,
        in_specs=placed,
        out_specs=(
            P(("dp", "mp"), None),
            P(("dp", "mp"), None),
            P("dp", "mp"),
            P(),
            P(),
            P(),
            P("dp", None, "mp"),
            P("mp", "dp"),
            P(),
            P(),
            P(),
            P("dp", "mp"),
            P("mp", "dp"),
            P(),
        ),
        check_vma=False,
    )
```

profile of v0, /device:TPU:0, one launch (start us, length us, event | category | flops | bytes accessed | tf_op | source)
XLA Modules:
  0.0 1000.9 jit_solution(7275968648900086361)
XLA Ops:
  15.8 6.2 gather_fusion
  22.6 26.2 %all_to_all.29 = f32[4,256,192]{1,2,0:T(8,128)S(1)} all-to-all(f32[4,256,192]{1,2,0:T(8,128)S(1)} %broadcast_add_fusion), channel_id=1, replica_groups=mesh['dp'=8,'mp'=4] {'mp'}, dimensions={0} | all-to-all | bytes 1572864 | tf_op jit(solution)/shard_map/all_to_all | solution.py:216
  52.8 34.0 %all-gather.13.cloned.1.call-done = bf16[1024,768]{1,0:T(8,128)(2,1)} async-done(((bf16[256,768]{1,0:T(8,128)(2,1)}), bf16[1024,768]{1,0:T(8,128)(2,1)}) %all-gather.13.cloned.1.call-update) | async-done | bytes 1572880 | tf_op jit(solution)/shard_map/all_gather | solution.py:115
  104.4 58.2 %reduce-scatter.17.cloned.1.call-done = f32[256,768]{1,0:T(8,128)} async-done(((f32[1024,768]{1,0:T(8,128)}), f32[256,768]{1,0:T(8,128)}) %reduce-scatter.17.cloned.1.call-update) | async-done | bytes 786448 | tf_op jit(solution)/shard_map/reduce_scatter | solution.py:131
  165.4 36.5 %all-gather.11.cloned.1.call-done = bf16[1024,768]{1,0:T(8,128)(2,1)} async-done(((bf16[256,768]{1,0:T(8,128)(2,1)}), bf16[1024,768]{1,0:T(8,128)(2,1)}) %all-gather.11.cloned.1.call-update) | async-done | bytes 1572880 | tf_op jit(solution)/shard_map/all_gather | solution.py:248
  206.7 33.2 %all-gather.15.cloned.1.call-done = bf16[1024,768]{1,0:T(8,128)(2,1)} async-done(((bf16[256,768]{1,0:T(8,128)(2,1)}), bf16[1024,768]{1,0:T(8,128)(2,1)}) %all-gather.15.cloned.1.call-update) | async-done | bytes 1572880 | tf_op jit(solution)/shard_map/all_gather | solution.py:143
  239.9 6.5 fusion.16
  250.3 34.3 %reduce-scatter.19.cloned.1.call-done = bf16[256,768]{1,0:T(8,128)(2,1)} async-done(((bf16[1024,768]{1,0:T(8,128)(2,1)}), bf16[256,768]{1,0:T(8,128)(2,1)}) %reduce-scatter.19.cloned.1.call-update) | async-done | bytes 393232 | tf_op jit(solution)/shard_map/reduce_scatter | solution.py:254
  293.0 34.7 %all-gather.17.cloned.1.call-done = bf16[1024,768]{1,0:T(8,128)(2,1)} async-done(((bf16[256,768]{1,0:T(8,128)(2,1)}), bf16[1024,768]{1,0:T(8,128)(2,1)}) %all-gather.17.cloned.1.call-update) | async-done | bytes 1572880 | tf_op jit(solution)/shard_map/all_gather | solution.py:266
  351.4 31.9 %reduce-scatter.21.cloned.1.call-done = bf16[256,768]{1,0:T(8,128)(2,1)} async-done(((bf16[1024,768]{1,0:T(8,128)(2,1)}), bf16[256,768]{1,0:T(8,128)(2,1)}) %reduce-scatter.21.cloned.1.call-update) | async-done | bytes 393232 | tf_op jit(solution)/shard_map/reduce_scatter | solution.py:280
  391.0 35.7 %all-gather.7.cloned.1.call-done = bf16[1024,768]{1,0:T(8,128)(2,1)} async-done(((bf16[256,768]{1,0:T(8,128)(2,1)}), bf16[1024,768]{1,0:T(8,128)(2,1)}) %all-gather.7.cloned.1.call-update) | async-done | bytes 1572880 | tf_op jit(solution)/shard_map/all_gather | solution.py:115
  430.5 6.0 fusion.128
  436.5 6.0 fusion.129
  451.9 59.2 %reduce-scatter.13.cloned.1.call-done = f32[256,768]{1,0:T(8,128)} async-done(((f32[1024,768]{1,0:T(8,128)}), f32[256,768]{1,0:T(8,128)}) %reduce-scatter.13.cloned.1.call-update) | async-done | bytes 786448 | tf_op jit(solution)/shard_map/reduce_scatter | solution.py:131
  517.0 25.0 %all_to_all.30 = bf16[256,4,192]{0,2,1:T(8,128)(2,1)S(1)} all-to-all(bf16[256,4,192]{0,2,1:T(8,128)(2,1)S(1)} %bitcast.201), channel_id=1, replica_groups=mesh['dp'=8,'mp'=4] {'mp'}, dimensions={1} | all-to-all | bytes 786432 | tf_op jit(solution)/shard_map/all_to_all | solution.py:289
  543.4 10.3 %scatter_custom_fusion = f32[8192,192]{1,0:T(8,128)} fusion(s32[1024]{0:T(1024)} %get-tuple-element.151, f32[1024,192]{1,0:T(8,128)} %bitcast.204, f32[]{:T(128)} %constant.117.clone.1), kind=kCustom, calls=%fused_computation.31 | custom fusion | flops 196608 | bytes 6291968 | tf_op jit(solution)/shard_map/scatter-add | solution.py:293
  581.4 14.4 %reduce-scatter.31.cloned.1.call-done = f32[96,192]{1,0:T(8,128)} async-done(((f32[768,192]{1,0:T(8,128)}), f32[96,192]{1,0:T(8,128)}) %reduce-scatter.31.cloned.1.call-update) | async-done | bytes 73744
  597.6 40.3 %all-reduce = (f32[768]{0:T(1024)}, f32[768]{0:T(1024)}, f32[768]{0:T(1024)}, f32[768]{0:T(1024)}, f32[768]{0:T(1024)}, /*index=5*/f32[768]{0:T(1024)}) all-reduce(f32[768]{0:T(1024)S(1)} %copy-done.35, f32[768]{0:T(1024)S(1)} %copy-done.34, f32[768]{0:T(1024)S(1)} %copy-done.32, ...), channel_id=1, replica_groups=mesh['dp'=8,'mp'=4] {'dp','mp'}, use_global_device_ids=true, to_apply=%region_31.32 | all-reduce | flops 4608 | bytes 36864 | tf_op jit(solution)/shard_map/psum | solution.py:311
  637.9 33.2 %reduce-scatter.23.cloned.1.call-done = f32[1024,192]{1,0:T(8,128)} async-done(((f32[8192,192]{1,0:T(8,128)}), f32[1024,192]{1,0:T(8,128)}) %reduce-scatter.23.cloned.1.call-update) | async-done | bytes 786448 | tf_op jit(solution)/shard_map/reduce_scatter | solution.py:328
  673.6 35.3 %reduce-scatter.15.cloned.1.call-done = bf16[256,768]{1,0:T(8,128)(2,1)} async-done(((bf16[1024,768]{1,0:T(8,128)(2,1)}), bf16[256,768]{1,0:T(8,128)(2,1)}) %reduce-scatter.15.cloned.1.call-update) | async-done | bytes 393232 | tf_op jit(solution)/shard_map/reduce_scatter | solution.py:146
  710.7 43.8 %reduce-scatter.29.cloned.1.call-done = f32[768,96]{0,1:T(8,128)} async-done(((f32[768,768]{0,1:T(8,128)}), f32[768,96]{0,1:T(8,128)}) %reduce-scatter.29.cloned.1.call-update) | async-done | bytes 294928 | tf_op jit(solution)/shard_map/reduce_scatter | solution.py:327
  754.5 46.3 %reduce-scatter.27.cloned.1.call-done = f32[96,768]{1,0:T(8,128)} async-done(((f32[768,768]{1,0:T(8,128)}), f32[96,768]{1,0:T(8,128)}) %reduce-scatter.27.cloned.1.call-update) | async-done | bytes 294928 | tf_op jit(solution)/shard_map/reduce_scatter | solution.py:326
  800.8 46.7 %reduce-scatter.25.cloned.1.call-done = f32[96,3,192]{2,0,1:T(8,128)} async-done(((f32[768,3,192]{2,0,1:T(8,128)}), f32[96,3,192]{2,0,1:T(8,128)}) %reduce-scatter.25.cloned.1.call-update) | async-done | bytes 221200 | tf_op jit(solution)/shard_map/reduce_scatter | solution.py:324
  847.5 143.0 %all-reduce.3.cloned.1.call-done = f32[1000,768]{1,0:T(8,128)} async-done(((f32[1000,768]{1,0:T(8,128)}), f32[1000,768]{1,0:T(8,128)}) %all-reduce.3.cloned.1.call-update) | async-done | bytes 3072016 | tf_op jit(solution)/shard_map/psum | solution.py:311
  (223 shorter events, 138.2 us)
Async XLA Ops:
  7.2 232.7 %copy-start = (bf16[768,768]{1,0:T(8,128)(2,1)S(1)}, bf16[768,768]{1,0:T(8,128)(2,1)}, u32[]{:S(2)}) copy-start(bf16[768,768]{1,0:T(8,128)(2,1)} %param.28) | copy-start | bytes 3538948
  7.2 79.6 %all-gather.13.cloned.1.call-start = ((), (), s32[]{:S(2)}) async-start(), calls=%async_computation.17 | async-start | bytes 1966080 | tf_op jit(solution)/shard_map/all_gather | solution.py:115
  50.5 112.1 %reduce-scatter.17.cloned.1.call-start = ((), (), s32[]{:S(2)}) async-start(), calls=%async_computation.18 | async-start | bytes 3932160 | tf_op jit(solution)/shard_map/reduce_scatter | solution.py:131
  101.0 61.6 %copy-start.25 = (f32[768]{0:T(1024)S(1)}, f32[768]{0:T(1024)}, u32[]{:S(2)}) copy-start(f32[768]{0:T(1024)} %param.25) | copy-start | bytes 9220
  103.3 60.9 %copy-start.18 = (f32[768]{0:T(1024)S(1)}, f32[768]{0:T(1024)}, u32[]{:S(2)}) copy-start(f32[768]{0:T(1024)} %param.26) | copy-start | bytes 9220
  103.3 98.6 %all-gather.11.cloned.1.call-start = ((), (), s32[]{:S(2)}) async-start(), calls=%async_computation.16 | async-start | bytes 1966080 | tf_op jit(solution)/shard_map/all_gather | solution.py:248
  104.4 135.5 %all-gather.15.cloned.1.call-start = ((), (), s32[]{:S(2)}) async-start(), calls=%async_computation.19 | async-start | bytes 1966080 | tf_op jit(solution)/shard_map/all_gather | solution.py:143
  164.2 122.3 %copy-start.28 = (f32[256]{0:T(256)}, f32[256]{0:T(256)S(1)}, u32[]{:S(2)}) copy-start(f32[256]{0:T(256)S(1)} %fusion.104) | copy-start | bytes 3076
  165.2 119.4 %reduce-scatter.19.cloned.1.call-start = ((), (), s32[]{:S(2)}) async-start(), calls=%async_computation.20 | async-start | bytes 1966080 | tf_op jit(solution)/shard_map/reduce_scatter | solution.py:254
  250.3 77.4 %all-gather.17.cloned.1.call-start = ((), (), s32[]{:S(2)}) async-start(), calls=%async_computation.21 | async-start | bytes 1966080 | tf_op jit(solution)/shard_map/all_gather | solution.py:266
  291.5 91.8 %reduce-scatter.21.cloned.1.call-start = ((), (), s32[]{:S(2)}) async-start(), calls=%async_computation.22 | async-start | bytes 1966080 | tf_op jit(solution)/shard_map/reduce_scatter | solution.py:280
  349.0 77.7 %all-gather.7.cloned.1.call-start = ((), (), s32[]{:S(2)}) async-start(), calls=%async_computation.12 | async-start | bytes 1966080 | tf_op jit(solution)/shard_map/all_gather | solution.py:115
  390.5 120.6 %reduce-scatter.13.cloned.1.call-start = ((), (), s32[]{:S(2)}) async-start(), calls=%async_computation.13 | async-start | bytes 3932160 | tf_op jit(solution)/shard_map/reduce_scatter | solution.py:131
  451.8 60.9 %copy-start.27 = (f32[768]{0:T(1024)S(1)}, f32[768]{0:T(1024)}, u32[]{:S(2)}) copy-start(f32[768]{0:T(1024)} %param.27) | copy-start | bytes 9220
  451.9 61.9 %copy-start.4 = (bf16[1024,3,64]{0,2,1:T(8,128)(2,1)S(1)}, bf16[1024,3,64]{0,2,1:T(8,128)(2,1)}, u32[]{:S(2)}) copy-start(bf16[1024,3,64]{0,2,1:T(8,128)(2,1)} %copy-done.3) | copy-start | bytes 1179652
  451.9 106.3 %all-gather.9.cloned.1.call-start = ((), (), s32[]{:S(2)}) async-start(), calls=%async_computation.14 | async-start | bytes 1966080 | tf_op jit(solution)/shard_map/all_gather | solution.py:143
  513.7 82.2 %reduce-scatter.31.cloned.1.call-start = ((), (), s32[]{:S(2)}) async-start(), calls=%async_computation.28 | async-start | bytes 884736
  516.8 154.4 %reduce-scatter.23.cloned.1.call-start = ((), (), s32[]{:S(2)}) async-start(), calls=%async_computation.23 | async-start | bytes 9437184 | tf_op jit(solution)/shard_map/reduce_scatter | solution.py:328
  553.7 155.1 %reduce-scatter.15.cloned.1.call-start = ((), (), s32[]{:S(2)}) async-start(), calls=%async_computation.15 | async-start | bytes 1966080 | tf_op jit(solution)/shard_map/reduce_scatter | solution.py:146
  564.0 190.5 %reduce-scatter.29.cloned.1.call-start = ((), (), s32[]{:S(2)}) async-start(), calls=%async_computation.27 | async-start | bytes 2654208 | tf_op jit(solution)/shard_map/reduce_scatter | solution.py:327
  569.1 231.7 %reduce-scatter.27.cloned.1.call-start = ((), (), s32[]{:S(2)}) async-start(), calls=%async_computation.26 | async-start | bytes 2654208 | tf_op jit(solution)/shard_map/reduce_scatter | solution.py:326
  574.0 273.4 %reduce-scatter.25.cloned.1.call-start = ((), (), s32[]{:S(2)}) async-start(), calls=%async_computation.25 | async-start | bytes 2654208 | tf_op jit(solution)/shard_map/reduce_scatter | solution.py:324
  578.8 411.6 %all-reduce.3.cloned.1.call-start = ((), (), s32[]{:S(2)}) async-start(), calls=%async_computation.24 | async-start | bytes 6144000 | tf_op jit(solution)/shard_map/psum | solution.py:311
  581.4 127.4 %copy-start.38 = (f32[768]{0:T(1024)S(1)}, f32[768]{0:T(1024)}, u32[]{:S(2)}) copy-start(f32[768]{0:T(1024)} %param.30) | copy-start | bytes 9220
  (40 other events, 368.8 us)
Sparse Core Ops, SparseCore 0:
  50.6 36.1 all-gather.12
  103.5 59.0 reduce-scatter.16
  164.7 37.1 all-gather.10
  203.9 35.9 all-gather.14
  250.4 34.1 reduce-scatter.18
  291.6 36.0 all-gather.16
  349.1 34.1 reduce-scatter.20
  390.6 36.0 all-gather.6
  452.0 59.0 reduce-scatter.12
  513.8 44.3 all-gather.8
  561.9 33.9 reduce-scatter.30
  599.2 71.8 reduce-scatter.22
  673.5 35.2 reduce-scatter.14
  713.0 41.4 reduce-scatter.28
  758.3 42.4 reduce-scatter.26
  804.9 42.4 reduce-scatter.24
  853.4 137.0 all-reduce.2
where the time goes:
time: 1000 us
  waiting for transfers between devices  725 us (72%)
  blocking collectives  91.6 us (9%)
  matrix products  89.9 us (9%)
  other arithmetic  48.9 us (5%)
  local copies, waits for them, and re-layouts  28.3 us (3%)
  between operations  15.6 us (2%)
    psum x1, waiting for transfers between devices, on_device(): lax.psum((grad_time_table, grad_ln1_gain, grad_ln1_bias, grad_attn_bias,...  143 us
    reduce_scatter x2, waiting for transfers between devices, block_forward(): lax.psum_scatter(jnp.dot(lax.slice_in_dim(attended_flat, 0, own_rows * la...  117 us
    all_gather x2, waiting for transfers between devices, block_forward(): gathered_one = lax.all_gather(normed_one, 'mp', axis=0, tiled=True)  69.7 us
    reduce_scatter x1, waiting for transfers between devices, on_device(): lax.psum_scatter(grad_w_qkv, 'dp', scatter_dimension=0, tiled=True)  46.7 us
    reduce_scatter x1, waiting for transfers between devices, on_device(): lax.psum_scatter(grad_w_up, 'dp', scatter_dimension=0, tiled=True)  46.3 us
    reduce_scatter x1, waiting for transfers between devices, on_device(): lax.psum_scatter(grad_w_down, 'dp', scatter_dimension=1, tiled=True)  43.8 us
    psum x1, blocking collectives, on_device(): lax.psum((grad_time_table, grad_ln1_gain, grad_ln1_bias, grad_attn_bias,...  40.3 us
    all_gather x2, waiting for transfers between devices, block_forward(): gathered_two = lax.all_gather(normed_two, 'mp', axis=0, tiled=True)  37.6 us
  transfers between devices with their start and end apart: 17, of which 17 were waited for; matrix products, arithmetic and copies ran while one was open for 6% of the time, Pallas kernels for 0%

commit v1 on v0

--- a/solution.py
+++ b/solution.py
@@ -1,3 +1,4 @@
+import functools
 import jax
 import jax.numpy as jnp
 from jax import lax
@@ -8,6 +9,14 @@
 L = 1024
 QBLK = 512
 PRECISE = lax.Precision.HIGHEST
+
+
+def tiles_render(arr, comm_axis, along_axis):
+    passed = lax.psum(arr, axis_name=comm_axis)
+    return lax.psum(passed, axis_name=along_axis)
+
+
+name_spots_for = functools.partial(tiles_render, comm_axis="mp", along_axis="dp")
 
 
 def as_sent(array):
@@ -308,7 +317,7 @@
         precision=PRECISE,
         preferred_element_type=jnp.float32,
     )
-    small_sums = lax.psum(
+    small_sums = name_spots_for(
         (
             grad_time_table,
             grad_ln1_gain,
@@ -317,8 +326,7 @@
             grad_ln2_gain,
             grad_ln2_bias,
             grad_mlp_bias,
-        ),
-        ("dp", "mp"),
+        )
     )
     sum_qkv, sum_out, sum_up, sum_down, sum_token = (
         lax.psum_scatter(grad_w_qkv, "dp", scatter_dimension=0, tiled=True),

time: 1000 us -> 1060 us (1.060)
  waiting for transfers between devices: 725 us -> 772 us
    psum x1 -> x2, waiting for transfers between devices: 143 us -> 172 us  [the longest x1 99.7 us: tiles_render(): passed = lax.psum(arr, axis_name=comm_axis)]
    unnamed x18 -> x19, waiting for transfers between devices: 14.7 us -> 38.2 us
    psum x1 -> x2, blocking collectives: 40.3 us -> 42.4 us  [the longest x1 23.5 us: tiles_render(): return lax.psum(passed, axis_name=along_axis)]
  transfers between devices with their start and end apart: 17 -> 18, of which waited for: 17 -> 18; matrix products, arithmetic and copies ran while one was open for 6% -> 5% of each run, Pallas kernels for 0% -> 0%
where the time goes in v1:
time: 1060 us; the launch traced here: 1050 us
  waiting for transfers between devices  772 us (73%)
  blocking collectives  95.4 us (9%)
  matrix products  90.2 us (9%)
  other arithmetic  48.9 us (5%)
  local copies, waits for them, and re-layouts  28.2 us (3%)
  between operations  16 us (2%)
    reduce_scatter x2, waiting for transfers between devices, block_forward(): lax.psum_scatter(jnp.dot(lax.slice_in_dim(attended_flat, 0, own_rows * la...  117 us
    psum x1, waiting for transfers between devices, tiles_render(): passed = lax.psum(arr, axis_name=comm_axis)  99.7 us
    psum x1, waiting for transfers between devices, tiles_render(): return lax.psum(passed, axis_name=along_axis)  72.6 us
    all_gather x2, waiting for transfers between devices, block_forward(): gathered_one = lax.all_gather(normed_one, 'mp', axis=0, tiled=True)  69.7 us
    reduce_scatter x1, waiting for transfers between devices, on_device(): lax.psum_scatter(grad_w_up, 'dp', scatter_dimension=0, tiled=True)  46.7 us
    reduce_scatter x1, waiting for transfers between devices, on_device(): lax.psum_scatter(grad_w_qkv, 'dp', scatter_dimension=0, tiled=True)  46.3 us
    reduce_scatter x1, waiting for transfers between devices, on_device(): lax.psum_scatter(grad_w_down, 'dp', scatter_dimension=1, tiled=True)  43.4 us
    unnamed x19, waiting for transfers between devices  38.2 us
  transfers between devices with their start and end apart: 18, of which 18 were waited for; matrix products, arithmetic and copies ran while one was open for 5% of the time, Pallas kernels for 0%

profile of v1, /device:TPU:0, one launch (start us, length us, event | category | flops | bytes accessed | tf_op | source)
XLA Modules:
  0.0 1052.4 jit_solution(15994189158337968531)
XLA Ops:
  15.8 6.2 gather_fusion
  22.6 26.2 %all_to_all.29 = f32[4,256,192]{1,2,0:T(8,128)S(1)} all-to-all(f32[4,256,192]{1,2,0:T(8,128)S(1)} %broadcast_add_fusion), channel_id=1, replica_groups=mesh['dp'=8,'mp'=4] {'mp'}, dimensions={0} | all-to-all | bytes 1572864 | tf_op jit(solution)/shard_map/all_to_all | solution.py:225
  52.8 34.0 %all-gather.13.cloned.1.call-done = bf16[1024,768]{1,0:T(8,128)(2,1)} async-done(((bf16[256,768]{1,0:T(8,128)(2,1)}), bf16[1024,768]{1,0:T(8,128)(2,1)}) %all-gather.13.cloned.1.call-update) | async-done | bytes 1572880 | tf_op jit(solution)/shard_map/all_gather | solution.py:124
  104.5 58.2 %reduce-scatter.17.cloned.1.call-done = f32[256,768]{1,0:T(8,128)} async-done(((f32[1024,768]{1,0:T(8,128)}), f32[256,768]{1,0:T(8,128)}) %reduce-scatter.17.cloned.1.call-update) | async-done | bytes 786448 | tf_op jit(solution)/shard_map/reduce_scatter | solution.py:140
  165.5 36.5 %all-gather.11.cloned.1.call-done = bf16[1024,768]{1,0:T(8,128)(2,1)} async-done(((bf16[256,768]{1,0:T(8,128)(2,1)}), bf16[1024,768]{1,0:T(8,128)(2,1)}) %all-gather.11.cloned.1.call-update) | async-done | bytes 1572880 | tf_op jit(solution)/shard_map/all_gather | solution.py:257
  206.8 33.2 %all-gather.15.cloned.1.call-done = bf16[1024,768]{1,0:T(8,128)(2,1)} async-done(((bf16[256,768]{1,0:T(8,128)(2,1)}), bf16[1024,768]{1,0:T(8,128)(2,1)}) %all-gather.15.cloned.1.call-update) | async-done | bytes 1572880 | tf_op jit(solution)/shard_map/all_gather | solution.py:152
  240.0 6.5 fusion.16
  250.4 34.2 %reduce-scatter.19.cloned.1.call-done = bf16[256,768]{1,0:T(8,128)(2,1)} async-done(((bf16[1024,768]{1,0:T(8,128)(2,1)}), bf16[256,768]{1,0:T(8,128)(2,1)}) %reduce-scatter.19.cloned.1.call-update) | async-done | bytes 393232 | tf_op jit(solution)/shard_map/reduce_scatter | solution.py:263
  293.0 34.7 %all-gather.17.cloned.1.call-done = bf16[1024,768]{1,0:T(8,128)(2,1)} async-done(((bf16[256,768]{1,0:T(8,128)(2,1)}), bf16[1024,768]{1,0:T(8,128)(2,1)}) %all-gather.17.cloned.1.call-update) | async-done | bytes 1572880 | tf_op jit(solution)/shard_map/all_gather | solution.py:275
  351.5 31.9 %reduce-scatter.21.cloned.1.call-done = bf16[256,768]{1,0:T(8,128)(2,1)} async-done(((bf16[1024,768]{1,0:T(8,128)(2,1)}), bf16[256,768]{1,0:T(8,128)(2,1)}) %reduce-scatter.21.cloned.1.call-update) | async-done | bytes 393232 | tf_op jit(solution)/shard_map/reduce_scatter | solution.py:289
  391.1 35.7 %all-gather.7.cloned.1.call-done = bf16[1024,768]{1,0:T(8,128)(2,1)} async-done(((bf16[256,768]{1,0:T(8,128)(2,1)}), bf16[1024,768]{1,0:T(8,128)(2,1)}) %all-gather.7.cloned.1.call-update) | async-done | bytes 1572880 | tf_op jit(solution)/shard_map/all_gather | solution.py:124
  452.1 59.2 %reduce-scatter.13.cloned.1.call-done = f32[256,768]{1,0:T(8,128)} async-done(((f32[1024,768]{1,0:T(8,128)}), f32[256,768]{1,0:T(8,128)}) %reduce-scatter.13.cloned.1.call-update) | async-done | bytes 786448 | tf_op jit(solution)/shard_map/reduce_scatter | solution.py:140
  519.6 26.8 %all_to_all.30 = bf16[256,4,192]{0,2,1:T(8,128)(2,1)S(1)} all-to-all(bf16[256,4,192]{0,2,1:T(8,128)(2,1)S(1)} %bitcast.201), channel_id=1, replica_groups=mesh['dp'=8,'mp'=4] {'mp'}, dimensions={1} | all-to-all | bytes 786432 | tf_op jit(solution)/shard_map/all_to_all | solution.py:298
  547.8 10.3 scatter_custom_fusion
  580.4 99.7 %all-reduce.5.cloned.1.call-done = f32[1000,768]{1,0:T(8,128)} async-done(((f32[1000,768]{1,0:T(8,128)}), f32[1000,768]{1,0:T(8,128)}) %all-reduce.5.cloned.1.call-update) | async-done | bytes 3072016 | tf_op jit(solution)/shard_map/psum | solution.py:15
  680.1 37.9 %reduce-scatter.31.cloned.1.call-done = f32[96,192]{1,0:T(8,128)} async-done(((f32[768,192]{1,0:T(8,128)}), f32[96,192]{1,0:T(8,128)}) %reduce-scatter.31.cloned.1.call-update) | async-done | bytes 73744
  719.7 18.9 %all-reduce.1 = (f32[768]{0:T(1024)S(1)}, f32[768]{0:T(1024)S(1)}, f32[768]{0:T(1024)S(1)}, f32[768]{0:T(1024)S(1)}, f32[768]{0:T(1024)S(1)}, /*index=5*/f32[768]{0:T(1024)S(1)}) all-reduce(f32[768]{0:T(1024)S(1)} %copy-done.36, f32[768]{0:T(1024)S(1)} %copy-done.35, f32[768]{0:T(1024)S(1)} %copy-done.33, ...), channel_id=1, replica_groups=mesh['dp'=8,'mp'=4] {'mp'}, use_global_device_ids=true, to_apply=%region_32.33 | all-reduce | flops 4608 | bytes 36864 | tf_op jit(solution)/shard_map/psum | solution.py:15
  738.6 23.5 %all-reduce = (f32[768]{0:T(1024)}, f32[768]{0:T(1024)}, f32[768]{0:T(1024)}, f32[768]{0:T(1024)}, f32[768]{0:T(1024)}, /*index=5*/f32[768]{0:T(1024)}) all-reduce(f32[768]{0:T(1024)S(1)} %get-tuple-element.139, f32[768]{0:T(1024)S(1)} %get-tuple-element.140, ...), channel_id=1, replica_groups=mesh['dp'=8,'mp'=4] {'dp'}, use_global_device_ids=true, to_apply=%region_33.34 | all-reduce | flops 4608 | bytes 36864 | tf_op jit(solution)/shard_map/psum | solution.py:16
  762.1 31.3 %reduce-scatter.23.cloned.1.call-done = f32[1024,192]{1,0:T(8,128)} async-done(((f32[8192,192]{1,0:T(8,128)}), f32[1024,192]{1,0:T(8,128)}) %reduce-scatter.23.cloned.1.call-update) | async-done | bytes 786448 | tf_op jit(solution)/shard_map/reduce_scatter | solution.py:336
  795.8 35.1 %reduce-scatter.15.cloned.1.call-done = bf16[256,768]{1,0:T(8,128)(2,1)} async-done(((bf16[1024,768]{1,0:T(8,128)(2,1)}), bf16[256,768]{1,0:T(8,128)(2,1)}) %reduce-scatter.15.cloned.1.call-update) | async-done | bytes 393232 | tf_op jit(solution)/shard_map/reduce_scatter | solution.py:155
  832.7 43.4 %reduce-scatter.29.cloned.1.call-done = f32[768,96]{0,1:T(8,128)} async-done(((f32[768,768]{0,1:T(8,128)}), f32[768,96]{0,1:T(8,128)}) %reduce-scatter.29.cloned.1.call-update) | async-done | bytes 294928 | tf_op jit(solution)/shard_map/reduce_scatter | solution.py:335
  876.1 46.7 %reduce-scatter.27.cloned.1.call-done = f32[96,768]{1,0:T(8,128)} async-done(((f32[768,768]{1,0:T(8,128)}), f32[96,768]{1,0:T(8,128)}) %reduce-scatter.27.cloned.1.call-update) | async-done | bytes 294928 | tf_op jit(solution)/shard_map/reduce_scatter | solution.py:334
  922.8 46.3 %reduce-scatter.25.cloned.1.call-done = f32[96,3,192]{2,0,1:T(8,128)} async-done(((f32[768,3,192]{2,0,1:T(8,128)}), f32[96,3,192]{2,0,1:T(8,128)}) %reduce-scatter.25.cloned.1.call-update) | async-done | bytes 221200 | tf_op jit(solution)/shard_map/reduce_scatter | solution.py:332
  969.1 72.6 %all-reduce.7.cloned.1.call-done = f32[1000,768]{1,0:T(8,128)} async-done(((f32[1000,768]{1,0:T(8,128)}), f32[1000,768]{1,0:T(8,128)}) %all-reduce.7.cloned.1.call-update) | async-done | bytes 3072016 | tf_op jit(solution)/shard_map/psum | solution.py:16
  (229 shorter events, 147.4 us)
Async XLA Ops:
  7.2 232.8 %copy-start = (bf16[768,768]{1,0:T(8,128)(2,1)S(1)}, bf16[768,768]{1,0:T(8,128)(2,1)}, u32[]{:S(2)}) copy-start(bf16[768,768]{1,0:T(8,128)(2,1)} %param.28) | copy-start | bytes 3538948
  7.2 79.6 %all-gather.13.cloned.1.call-start = ((), (), s32[]{:S(2)}) async-start(), calls=%async_computation.17 | async-start | bytes 1966080 | tf_op jit(solution)/shard_map/all_gather | solution.py:124
  50.5 112.2 %reduce-scatter.17.cloned.1.call-start = ((), (), s32[]{:S(2)}) async-start(), calls=%async_computation.18 | async-start | bytes 3932160 | tf_op jit(solution)/shard_map/reduce_scatter | solution.py:140
  103.4 98.6 %all-gather.11.cloned.1.call-start = ((), (), s32[]{:S(2)}) async-start(), calls=%async_computation.16 | async-start | bytes 1966080 | tf_op jit(solution)/shard_map/all_gather | solution.py:257
  104.5 135.5 %all-gather.15.cloned.1.call-start = ((), (), s32[]{:S(2)}) async-start(), calls=%async_computation.19 | async-start | bytes 1966080 | tf_op jit(solution)/shard_map/all_gather | solution.py:152
  165.3 119.4 %reduce-scatter.19.cloned.1.call-start = ((), (), s32[]{:S(2)}) async-start(), calls=%async_computation.20 | async-start | bytes 1966080 | tf_op jit(solution)/shard_map/reduce_scatter | solution.py:263
  250.4 77.4 %all-gather.17.cloned.1.call-start = ((), (), s32[]{:S(2)}) async-start(), calls=%async_computation.21 | async-start | bytes 1966080 | tf_op jit(solution)/shard_map/all_gather | solution.py:275
  291.5 91.8 %reduce-scatter.21.cloned.1.call-start = ((), (), s32[]{:S(2)}) async-start(), calls=%async_computation.22 | async-start | bytes 1966080 | tf_op jit(solution)/shard_map/reduce_scatter | solution.py:289
  349.1 77.7 %all-gather.7.cloned.1.call-start = ((), (), s32[]{:S(2)}) async-start(), calls=%async_computation.12 | async-start | bytes 1966080 | tf_op jit(solution)/shard_map/all_gather | solution.py:124
  390.6 120.7 %reduce-scatter.13.cloned.1.call-start = ((), (), s32[]{:S(2)}) async-start(), calls=%async_computation.13 | async-start | bytes 3932160 | tf_op jit(solution)/shard_map/reduce_scatter | solution.py:140
  452.0 107.5 %all-gather.9.cloned.1.call-start = ((), (), s32[]{:S(2)}) async-start(), calls=%async_computation.14 | async-start | bytes 1966080 | tf_op jit(solution)/shard_map/all_gather | solution.py:152
  513.8 166.3 %all-reduce.5.cloned.1.call-start = ((), (), s32[]{:S(2)}) async-start(), calls=%async_computation.24 | async-start | bytes 6144000 | tf_op jit(solution)/shard_map/psum | solution.py:15
  516.3 201.7 %reduce-scatter.31.cloned.1.call-start = ((), (), s32[]{:S(2)}) async-start(), calls=%async_computation.29 | async-start | bytes 884736
  519.4 274.0 %reduce-scatter.23.cloned.1.call-start = ((), (), s32[]{:S(2)}) async-start(), calls=%async_computation.23 | async-start | bytes 9437184 | tf_op jit(solution)/shard_map/reduce_scatter | solution.py:336
  558.1 272.7 %reduce-scatter.15.cloned.1.call-start = ((), (), s32[]{:S(2)}) async-start(), calls=%async_computation.15 | async-start | bytes 1966080 | tf_op jit(solution)/shard_map/reduce_scatter | solution.py:155
  565.3 310.8 %reduce-scatter.29.cloned.1.call-start = ((), (), s32[]{:S(2)}) async-start(), calls=%async_computation.28 | async-start | bytes 2654208 | tf_op jit(solution)/shard_map/reduce_scatter | solution.py:335
  571.0 351.8 %reduce-scatter.27.cloned.1.call-start = ((), (), s32[]{:S(2)}) async-start(), calls=%async_computation.27 | async-start | bytes 2654208 | tf_op jit(solution)/shard_map/reduce_scatter | solution.py:334
  575.9 393.1 %reduce-scatter.25.cloned.1.call-start = ((), (), s32[]{:S(2)}) async-start(), calls=%async_computation.26 | async-start | bytes 2654208 | tf_op jit(solution)/shard_map/reduce_scatter | solution.py:332
  580.3 139.3 %copy-start.33 = (f32[768]{0:T(1024)S(1)}, f32[768]{0:T(1024)}, u32[]{:S(2)}) copy-start(f32[768]{0:T(1024)} %get-tuple-element.145) | copy-start | bytes 9220
  580.3 139.3 %copy-start.34 = (f32[768]{0:T(1024)S(1)}, f32[768]{0:T(1024)}, u32[]{:S(2)}) copy-start(f32[768]{0:T(1024)} %get-tuple-element.154) | copy-start | bytes 9220
  580.3 139.4 %copy-start.35 = (f32[768]{0:T(1024)S(1)}, f32[768]{0:T(1024)}, u32[]{:S(2)}) copy-start(f32[768]{0:T(1024)} %get-tuple-element.131) | copy-start | bytes 9220
  580.3 139.4 %copy-start.36 = (f32[768]{0:T(1024)S(1)}, f32[768]{0:T(1024)}, u32[]{:S(2)}) copy-start(f32[768]{0:T(1024)} %get-tuple-element.127) | copy-start | bytes 9220
  580.3 250.5 %copy-start.39 = (f32[768]{0:T(1024)S(1)}, f32[768]{0:T(1024)}, u32[]{:S(2)}) copy-start(f32[768]{0:T(1024)} %param.30) | copy-start | bytes 9220
  580.3 461.3 %all-reduce.7.cloned.1.call-start = ((), (), s32[]{:S(2)}) async-start(), calls=%async_computation.25 | async-start | bytes 6144000 | tf_op jit(solution)/shard_map/psum | solution.py:16
  (42 other events, 966.5 us)
Sparse Core Ops, SparseCore 0:
  50.6 36.1 all-gather.12
  103.5 59.1 reduce-scatter.16
  164.8 37.0 all-gather.10
  204.0 35.9 all-gather.14
  250.5 34.1 reduce-scatter.18
  291.6 36.0 all-gather.16
  349.2 34.1 reduce-scatter.20
  390.7 36.0 all-gather.6
  452.1 59.1 reduce-scatter.12
  513.9 45.5 all-gather.8
  562.5 117.5 all-reduce.4
  684.0 33.9 reduce-scatter.30
  721.8 71.4 reduce-scatter.22
  795.5 35.2 reduce-scatter.14
  834.6 41.4 reduce-scatter.28
  880.2 42.4 reduce-scatter.26
  926.5 42.4 reduce-scatter.24
  972.6 68.9 all-reduce.6
